TPU v7x, 32 devices: a whole 2x2x4 slice. The times are simulated.
32 devices in a mesh: batch: 4 (over x, core), centers: 8 (over z, y).
Axes of the slice: x: 2, y: 2, z: 4, core: 2. Of those that a mesh axis runs over, the one named last changes fastest.
Arguments:
- pool_features: float32 [32768, 128], P(('batch', 'centers')), may hold values from -14 to 14
- pool_targets: float32 [32768, 64], P(('batch', 'centers')), may hold values from -6 to 6
- batch_index: int32 [2048], P(('batch', 'centers')), may hold values from 0 to 1023
- centers: float32 [4096, 128], P('centers'), may hold values from -14 to 14
- weights: float32 [4096, 64], P('centers'), as said below
- eig_vectors: float32 [4096, 1024], P(('batch', 'centers')), may hold values from -0.09375 to 0.09375
- eig_scale: float32 [1024], replicated, may hold values from 0.5 to 4
- nys_owner: int32 [4096, 1], P(('batch', 'centers')), may hold values from 0 to 7; in each aligned block of 128 rows (0 to 127, 128 to 255, ...) at most 32 rows name the same one
- nys_offset: int32 [4096], P(('batch', 'centers')), may hold values from 0 to 511
Outputs:
- residual_out: float32 [2048, 64], P(('batch', 'centers'))
- update: float32 [4096, 64], P('centers')
Inputs may be any that keep to these rules, and one draw needn't show every extreme that they name: `nys_owner`: among the 128 rows of one device no owner is named more than 32 times; on some devices one owner is named exactly 32 times. `weights`: every column sums to zero.
All inputs are finite; a program needn't handle non-finite values.
Results may differ from a plain program's by a relative error of at most 0.0003.
Values sent between devices are 32-bit elements; how exact they have to be, the bound alone decides.
A program may use at most 64 MiB of HBM per device.

v0:
```python
import math
import jax
import jax.numpy as jnp
from jax import lax
from jax.sharding import PartitionSpec as P

DEPTH = 3
epsilon = 1e-06
highest = lax.Precision.HIGHEST


def kernel_rows(row_block, center_block, center_norm):
    inner_prod = (
        lax.dot_general(
            row_block,
            center_block,
            (((1,), (1,)), ((), ())),
            precision=highest,
            preferred_element_type=jnp.float32,
        )
        / row_block.shape[1]
    )
    row_norm = jnp.mean(row_block * row_block, axis=1) + epsilon
    norm_scale = jnp.sqrt(row_norm[:, None] * center_norm[None, :])
    sigma_now = inner_prod
    tangent = inner_prod
    for depth_step in range(DEPTH):
        cosine = sigma_now / norm_scale
        arc_angle = jnp.arccos(cosine)
        remain = (math.pi - arc_angle) / math.pi
        sigma_now = (
            norm_scale
            * (jnp.sqrt(1.0 - cosine * cosine) + (math.pi - arc_angle) * cosine)
            / math.pi
        )
        tangent = sigma_now + tangent * remain
    return tangent


def per_device(
    pool_features,
    pool_targets,
    batch_index,
    centers,
    weights,
    eig_vectors,
    eig_scale,
    nys_owner,
    nys_offset,
):
    local_rows = pool_features[batch_index]
    local_targets = pool_targets[batch_index]
    row_count = local_rows.shape[0]
    group_size = lax.axis_size("centers")
    rows_total = row_count * group_size * lax.axis_size("batch")
    center_count = centers.shape[0]
    outputs = weights.shape[1]
    center_norm = jnp.mean(centers * centers, axis=1) + epsilon
    kernel = kernel_rows(
        lax.all_gather(local_rows, "centers", axis=0, tiled=True), centers, center_norm
    )
    partial_pred = jnp.dot(kernel, weights, precision=highest, preferred_element_type=jnp.float32)
    all_targets = lax.all_gather(local_targets, "centers", axis=0, tiled=True)
    prediction = lax.psum(partial_pred, "centers")
    residual = prediction - all_targets
    own_residual = lax.dynamic_slice_in_dim(
        residual, lax.axis_index("centers") * row_count, row_count, 0
    )
    grads_part = lax.dot_general(
        kernel,
        residual,
        (((0,), (0,)), ((), ())),
        precision=highest,
        preferred_element_type=jnp.float32,
    ) / math.sqrt(rows_total)
    grads = lax.psum(grads_part, "batch")
    owner = nys_owner[:, 0]
    slots = max(2, 2 * owner.shape[0] // group_size)
    owner_hot = (owner[:, None] == jnp.arange(group_size, dtype=jnp.int32)[None, :]).astype(
        jnp.int32
    )
    slot_rank = jnp.sum((jnp.cumsum(owner_hot, axis=0) - owner_hot) * owner_hot, axis=1)
    requests = jnp.zeros((group_size, slots), jnp.int32).at[owner, slot_rank].set(nys_offset)
    received = lax.all_to_all(requests, "centers", split_axis=0, concat_axis=0, tiled=True)
    found = grads[received]
    returned = lax.all_to_all(found, "centers", split_axis=0, concat_axis=0, tiled=True)
    picked_grads = returned[owner, slot_rank]
    coeff_part = lax.dot_general(
        eig_vectors,
        picked_grads,
        (((0,), (0,)), ((), ())),
        precision=highest,
        preferred_element_type=jnp.float32,
    )
    coeff = lax.psum(coeff_part, ("batch", "centers"))
    corr_rows = jnp.dot(
        eig_vectors,
        eig_scale[:, None] * coeff,
        precision=highest,
        preferred_element_type=jnp.float32,
    )
    outgoing = (
        jnp.zeros((group_size, slots, outputs), jnp.float32).at[owner, slot_rank].set(corr_rows)
    )
    incoming = lax.all_to_all(outgoing, "centers", split_axis=0, concat_axis=0, tiled=True)
    corr_part = jnp.zeros((center_count, outputs), jnp.float32).at[received].add(incoming)
    correction = lax.psum(corr_part, "batch")
    return (own_residual, correction - grads)


def solution(mesh):
    placed = (
        P(("batch", "centers"), None),
        P(("batch", "centers"), None),
        P(("batch", "centers")),
        P("centers", None),
        P("centers", None),
        P(("batch", "centers"), None),
        P(),
        P(("batch", "centers"), None),
        P(("batch", "centers")),
    )
    return jax.shard_map(
        per_device,
        mesh=mesh,
        in_specs=placed,
        out_specs=(P(("batch", "centers"), None), P("centers", None)),
        check_vma=False,
    )
```

profile of v0, /device:TPU:0, one launch (start us, length us, event | category | flops | bytes accessed | tf_op | source)
XLA Modules:
  0.0 387.0 jit_solution(5106888059048131326)
XLA Ops:
  9.0 19.9 %scatter_fusion = s32[8,32]{1,0:T(8,128)} fusion(s32[8,32]{1,0:T(8,128)} %broadcast.104, s32[128]{0:T(128)S(1)} %get-tuple-element.8, s32[128]{0:T(128)S(1)} %copy-done.8), kind=kCustom, calls=%fused_computation.4 | custom fusion | bytes 2560 | tf_op jit(solution)/shard_map/scatter | solution.py:83
  28.9 7.4 %all-to-all-start = ((s32[8,1,32]{2,1,0:T(1,128)}), s32[8,1,32]{2,1,0:T(1,128)S(1)}, u32[]{:S(2)}, u32[]{:S(2)}) async-start(s32[8,1,32]{2,1,0:T(1,128)} %bitcast.4), calls=%async_computation | async-start | bytes 8192 | tf_op jit(solution)/shard_map/all_to_all | solution.py:84
  37.2 31.2 %all-gather = f32[512,128]{1,0:T(8,128)S(1)} all-gather(f32[64,128]{1,0:T(8,128)S(1)} %gather_fusion), channel_id=2, replica_groups=mesh['batch'=4,'centers'=8] {'centers'}, dimensions={0}, use_global_device_ids=true | all-gather | bytes 294912 | tf_op jit(solution)/shard_map/all_gather | solution.py:60
  68.6 8.9 %multiply_add_fusion = f32[512,512]{1,0:T(8,128)S(1)} fusion(f32[512,128]{1,0:T(8,128)S(1)} %all-gather, f32[512,128]{1,0:T(8,128)S(1)} %copy-done.3, f32[512]{0:T(512)S(1)} %multiply_add_fusion.1, f32[512]{0:T(512)S(1)} %multiply_add_fusion.2), kind=kOutput, calls=%fused_computation.11 | convolution fusion | flops 414187520 | bytes 1576960 | tf_op jit(solution)/shard_map/dot_general | solution.py:14
  77.5 1.8 fusion.8
  80.2 30.8 %all-gather.1 = f32[512,64]{1,0:T(8,128)S(1)} all-gather(f32[64,64]{1,0:T(8,128)S(1)} %gather_fusion.1), channel_id=3, replica_groups=mesh['batch'=4,'centers'=8] {'centers'}, dimensions={0}, use_global_device_ids=true | all-gather | bytes 147456 | tf_op jit(solution)/shard_map/all_gather | solution.py:63
  111.3 39.5 %all-reduce.5.cloned.1.call-done = f32[512,64]{0,1:T(8,128)} async-done(((f32[512,64]{0,1:T(8,128)}), f32[512,64]{0,1:T(8,128)}) %all-reduce.5.cloned.1.call-update) | async-done | bytes 131088 | tf_op jit(solution)/shard_map/psum | solution.py:64
  150.8 0.9 sub.36
  151.7 1.5 convolution_multiply_fusion.1
  153.3 31.3 %all-reduce.7.cloned.1.call-done = f32[512,64]{0,1:T(8,128)} async-done(((f32[512,64]{0,1:T(8,128)}), f32[512,64]{0,1:T(8,128)}) %all-reduce.7.cloned.1.call-update) | async-done | bytes 131088 | tf_op jit(solution)/shard_map/psum | solution.py:76
  184.6 1.0 copy.26
  186.5 12.2 %all_to_all.22 = f32[8,1,2048]{2,1,0:T(1,128)S(1)} all-to-all(f32[8,1,2048]{2,1,0:T(1,128)S(1)} %reshape.114), channel_id=1, replica_groups=mesh['batch'=4,'centers'=8] {'centers'}, dimensions={0} | all-to-all | bytes 131072 | tf_op jit(solution)/shard_map/all_to_all | solution.py:86
  199.2 0.8 reduce
  200.1 1.2 gather_fusion.3
  201.3 1.1 convolution_bitcast_fusion
  202.5 123.4 %all-reduce.9.cloned.1.call-done = f32[1024,64]{0,1:T(8,128)} async-done(((f32[1024,64]{0,1:T(8,128)}), f32[1024,64]{0,1:T(8,128)}) %all-reduce.9.cloned.1.call-update) | async-done | bytes 262160 | tf_op jit(solution)/shard_map/psum | solution.py:95
  325.9 1.6 convolution_bitcast_fusion.1
  327.7 6.9 %scatter_fusion.1 = f32[8,32,64]{2,1,0:T(8,128)S(1)} fusion(f32[8,32,64]{2,1,0:T(8,128)S(1)} %broadcast_in_dim.8, s32[128]{0:T(128)S(1)} %get-tuple-element.8, f32[128,64]{1,0:T(8,128)S(1)} %copy.27), kind=kCustom, calls=%fused_computation.5 | custom fusion | bytes 99328 | tf_op jit(solution)/shard_map/scatter | solution.py:103
  335.3 4.5 %all-to-all-start.2 = ((f32[8,1,2048]{2,1,0:T(1,128)}), f32[8,1,2048]{2,1,0:T(1,128)S(1)}, u32[]{:S(2)}, u32[]{:S(2)}) async-start(f32[8,1,2048]{2,1,0:T(1,128)} %reshape.116), calls=%async_computation.2 | async-start | bytes 131072 | tf_op jit(solution)/shard_map/all_to_all | solution.py:105
  339.9 6.9 %all-to-all-done.2 = f32[8,1,2048]{2,1,0:T(1,128)S(1)} async-done(((f32[8,1,2048]{2,1,0:T(1,128)}), f32[8,1,2048]{2,1,0:T(1,128)S(1)}, u32[]{:S(2)}, u32[]{:S(2)}) %all-to-all-start.2) | async-done | bytes 65568 | tf_op jit(solution)/shard_map/all_to_all | solution.py:105
  346.7 0.8 reduce.1
  347.6 1.7 scatter_custom_fusion.2
  351.0 27.9 %all-reduce.11.cloned.1.call-done = f32[512,64]{0,1:T(8,128)} async-done(((f32[512,64]{0,1:T(8,128)}), f32[512,64]{0,1:T(8,128)}) %all-reduce.11.cloned.1.call-update) | async-done | bytes 131088 | tf_op jit(solution)/shard_map/psum | solution.py:107
  378.9 1.6 sub.38
  (58 shorter events, 7.9 us)
Async XLA Ops:
  7.2 194.2 %copy-start = (f32[128,1024]{1,0:T(8,128)S(1)}, f32[128,1024]{1,0:T(8,128)}, u32[]{:S(2)}) copy-start(f32[128,1024]{1,0:T(8,128)} %param.14) | copy-start | bytes 1572868
  7.2 0.7 copy-start.6
  8.3 0.7 copy-start.8
  9.0 27.4 %copy-start.3 = (f32[512,128]{1,0:T(8,128)S(1)}, f32[512,128]{1,0:T(8,128)}, u32[]{:S(2)}) copy-start(f32[512,128]{1,0:T(8,128)} %param.12) | copy-start | bytes 786436
  9.0 27.6 %copy-start.5 = (f32[1024,128]{1,0:T(8,128)S(1)}, f32[1024,128]{1,0:T(8,128)}, u32[]{:S(2)}) copy-start(f32[1024,128]{1,0:T(8,128)} %param.9) | copy-start | bytes 1572868
  28.9 7.5 %copy-start.9 = (s32[64]{0:T(128)S(1)}, s32[64]{0:T(128)}, u32[]{:S(2)}) copy-start(s32[64]{0:T(128)} %param.11) | copy-start | bytes 772
  28.9 82.3 %all-to-all-start = ((s32[8,1,32]{2,1,0:T(1,128)}), s32[8,1,32]{2,1,0:T(1,128)S(1)}, u32[]{:S(2)}, u32[]{:S(2)}) async-start(s32[8,1,32]{2,1,0:T(1,128)} %bitcast.4), calls=%async_computation | async-start | bytes 8192 | tf_op jit(solution)/shard_map/all_to_all | solution.py:84
  36.3 114.5 %all-reduce.5.cloned.1.call-start = ((), (), s32[]{:S(2)}) async-start(), calls=%async_computation.3 | async-start | bytes 262144 | tf_op jit(solution)/shard_map/psum | solution.py:64
  68.6 8.9 %copy-start.4 = (f32[512,64]{0,1:T(8,128)S(1)}, f32[512,64]{0,1:T(8,128)}, u32[]{:S(2)}) copy-start(f32[512,64]{0,1:T(8,128)} %param.13) | copy-start | bytes 393220
  77.5 1.9 copy-start.2
  79.4 105.2 %all-reduce.7.cloned.1.call-start = ((), (), s32[]{:S(2)}) async-start(), calls=%async_computation.4 | async-start | bytes 262144 | tf_op jit(solution)/shard_map/psum | solution.py:76
  153.2 172.7 %all-reduce.9.cloned.1.call-start = ((), (), s32[]{:S(2)}) async-start(), calls=%async_computation.5 | async-start | bytes 524288 | tf_op jit(solution)/shard_map/psum | solution.py:95
  202.5 123.4 %copy-start.7 = (f32[1024]{0:T(1024)S(1)}, f32[1024]{0:T(1024)}, u32[]{:S(2)}) copy-start(f32[1024]{0:T(1024)} %param.15) | copy-start | bytes 12292
  335.3 11.4 %all-to-all-start.2 = ((f32[8,1,2048]{2,1,0:T(1,128)}), f32[8,1,2048]{2,1,0:T(1,128)S(1)}, u32[]{:S(2)}, u32[]{:S(2)}) async-start(f32[8,1,2048]{2,1,0:T(1,128)} %reshape.116), calls=%async_computation.2 | async-start | bytes 131072 | tf_op jit(solution)/shard_map/all_to_all | solution.py:105
  339.8 39.0 %all-reduce.11.cloned.1.call-start = ((), (), s32[]{:S(2)}) async-start(), calls=%async_computation.6 | async-start | bytes 262144 | tf_op jit(solution)/shard_map/psum | solution.py:107
  350.1 28.7 %copy-start.1 = (f32[512,64]{0,1:T(8,128)S(1)}, f32[512,64]{0,1:T(8,128)}, u32[]{:S(2)}) copy-start(f32[512,64]{0,1:T(8,128)} %all-reduce.7.cloned.1.call-done) | copy-start | bytes 393220
Sparse Core Ops, SparseCore 0:
  79.5 71.2 all-reduce.4
  153.7 30.8 all-reduce.6
  202.6 123.2 all-reduce.8
  350.3 28.5 all-reduce.10
where the time goes:
time: 388 us; the launch traced here: 387 us
  waiting for transfers between devices  229 us (59%)
  blocking collectives  74.3 us (19%)
  local copies, waits for them, and re-layouts  36 us (9%)
  matrix products  14.9 us (4%)
  between operations  14 us (4%)
  starting transfers between devices  12.1 us (3%)
  other arithmetic  6.6 us (2%)
    psum x1, waiting for transfers between devices, per_device(): coeff = lax.psum(coeff_part, ('batch', 'centers'))  123 us
    psum x1, waiting for transfers between devices, per_device(): prediction = lax.psum(partial_pred, 'centers')  39.5 us
    psum x1, waiting for transfers between devices, per_device(): grads = lax.psum(grads_part, 'batch')  31.3 us
    all_gather x1, blocking collectives, per_device(): lax.all_gather(local_rows, 'centers', axis=0, tiled=True)  31.2 us
    all_gather x1, blocking collectives, per_device(): all_targets = lax.all_gather(local_targets, 'centers', axis=0, tiled=True)  30.8 us
    psum x1, waiting for transfers between devices, per_device(): correction = lax.psum(corr_part, 'batch')  27.9 us
    scatter x1, local copies, waits for them, and re-layouts, per_device(): jnp.zeros((group_size, slots), jnp.int32).at[owner, slot_rank]  19.9 us
    all_to_all x1, blocking collectives, per_device(): lax.all_to_all(found, 'centers', split_axis=0, concat_axis=0, tiled=True)  12.2 us
  transfers between devices with their start and end apart: 6, of which 5 were waited for; matrix products, arithmetic and copies ran while one was open for 3% of the time, Pallas kernels for 0%

commit v1 on v0

--- a/solution.py
+++ b/solution.py
@@ -92,7 +92,7 @@
         precision=highest,
         preferred_element_type=jnp.float32,
     )
-    coeff = lax.psum(coeff_part, ("batch", "centers"))
+    coeff = lax.psum(lax.psum(coeff_part, "centers"), "batch")
     corr_rows = jnp.dot(
         eig_vectors,
         eig_scale[:, None] * coeff,

time: 388 us -> 367 us (0.946)
  waiting for transfers between devices: 229 us -> 207 us
    psum x1 -> x2, waiting for transfers between devices: 123 us -> 101 us  [per_device(): coeff = lax.psum(lax.psum(coeff_part, 'centers'), 'batch')]
  transfers between devices with their start and end apart: 6 -> 7, of which waited for: 5 -> 6; matrix products, arithmetic and copies ran while one was open for 3% -> 4% of each run, Pallas kernels for 0% -> 0%
where the time goes in v1:
time: 367 us; the launch traced here: 366 us
  waiting for transfers between devices  207 us (56%)
  blocking collectives  74.3 us (20%)
  local copies, waits for them, and re-layouts  36 us (10%)
  matrix products  14.9 us (4%)
  between operations  14 us (4%)
  starting transfers between devices  13.1 us (4%)
  other arithmetic  6.6 us (2%)
    psum x2, waiting for transfers between devices, per_device(): coeff = lax.psum(lax.psum(coeff_part, 'centers'), 'batch')  101 us
    psum x1, waiting for transfers between devices, per_device(): prediction = lax.psum(partial_pred, 'centers')  39.5 us
    psum x1, waiting for transfers between devices, per_device(): grads = lax.psum(grads_part, 'batch')  31.3 us
    all_gather x1, blocking collectives, per_device(): lax.all_gather(local_rows, 'centers', axis=0, tiled=True)  31.2 us
    all_gather x1, blocking collectives, per_device(): all_targets = lax.all_gather(local_targets, 'centers', axis=0, tiled=True)  30.8 us
    psum x1, waiting for transfers between devices, per_device(): correction = lax.psum(corr_part, 'batch')  27.9 us
    scatter x1, local copies, waits for them, and re-layouts, per_device(): jnp.zeros((group_size, slots), jnp.int32).at[owner, slot_rank]  19.9 us
    all_to_all x1, blocking collectives, per_device(): lax.all_to_all(found, 'centers', split_axis=0, concat_axis=0, tiled=True)  12.2 us
  transfers between devices with their start and end apart: 7, of which 6 were waited for; matrix products, arithmetic and copies ran while one was open for 4% of the time, Pallas kernels for 0%

profile of v1, /device:TPU:0, one launch (start us, length us, event | category | flops | bytes accessed | tf_op | source)
XLA Modules:
  0.0 366.0 jit_solution(8851267280370700177)
XLA Ops:
  9.0 19.9 %scatter_fusion = s32[8,32]{1,0:T(8,128)} fusion(s32[8,32]{1,0:T(8,128)} %broadcast.104, s32[128]{0:T(128)S(1)} %get-tuple-element.8, s32[128]{0:T(128)S(1)} %copy-done.8), kind=kCustom, calls=%fused_computation.4 | custom fusion | bytes 2560 | tf_op jit(solution)/shard_map/scatter | solution.py:83
  28.9 7.4 %all-to-all-start = ((s32[8,1,32]{2,1,0:T(1,128)}), s32[8,1,32]{2,1,0:T(1,128)S(1)}, u32[]{:S(2)}, u32[]{:S(2)}) async-start(s32[8,1,32]{2,1,0:T(1,128)} %bitcast.4), calls=%async_computation | async-start | bytes 8192 | tf_op jit(solution)/shard_map/all_to_all | solution.py:84
  37.2 31.2 %all-gather = f32[512,128]{1,0:T(8,128)S(1)} all-gather(f32[64,128]{1,0:T(8,128)S(1)} %gather_fusion), channel_id=2, replica_groups=mesh['batch'=4,'centers'=8] {'centers'}, dimensions={0}, use_global_device_ids=true | all-gather | bytes 294912 | tf_op jit(solution)/shard_map/all_gather | solution.py:60
  68.6 8.9 %multiply_add_fusion = f32[512,512]{1,0:T(8,128)S(1)} fusion(f32[512,128]{1,0:T(8,128)S(1)} %all-gather, f32[512,128]{1,0:T(8,128)S(1)} %copy-done.3, f32[512]{0:T(512)S(1)} %multiply_add_fusion.1, f32[512]{0:T(512)S(1)} %multiply_add_fusion.2), kind=kOutput, calls=%fused_computation.11 | convolution fusion | flops 414187520 | bytes 1576960 | tf_op jit(solution)/shard_map/dot_general | solution.py:14
  77.5 1.8 fusion.8
  80.2 30.8 %all-gather.1 = f32[512,64]{1,0:T(8,128)S(1)} all-gather(f32[64,64]{1,0:T(8,128)S(1)} %gather_fusion.1), channel_id=3, replica_groups=mesh['batch'=4,'centers'=8] {'centers'}, dimensions={0}, use_global_device_ids=true | all-gather | bytes 147456 | tf_op jit(solution)/shard_map/all_gather | solution.py:63
  111.3 39.5 %all-reduce.6.cloned.1.call-done = f32[512,64]{0,1:T(8,128)} async-done(((f32[512,64]{0,1:T(8,128)}), f32[512,64]{0,1:T(8,128)}) %all-reduce.6.cloned.1.call-update) | async-done | bytes 131088 | tf_op jit(solution)/shard_map/psum | solution.py:64
  150.8 0.9 sub.36
  151.7 1.5 convolution_multiply_fusion.1
  153.3 31.3 %all-reduce.8.cloned.1.call-done = f32[512,64]{0,1:T(8,128)} async-done(((f32[512,64]{0,1:T(8,128)}), f32[512,64]{0,1:T(8,128)}) %all-reduce.8.cloned.1.call-update) | async-done | bytes 131088 | tf_op jit(solution)/shard_map/psum | solution.py:76
  184.6 1.0 copy.26
  186.5 12.2 %all_to_all.22 = f32[8,1,2048]{2,1,0:T(1,128)S(1)} all-to-all(f32[8,1,2048]{2,1,0:T(1,128)S(1)} %reshape.114), channel_id=1, replica_groups=mesh['batch'=4,'centers'=8] {'centers'}, dimensions={0} | all-to-all | bytes 131072 | tf_op jit(solution)/shard_map/all_to_all | solution.py:86
  199.2 0.8 reduce
  200.1 1.2 gather_fusion.3
  201.3 1.1 convolution_bitcast_fusion
  202.5 67.7 %all-reduce.10.cloned.1.call-done = f32[1024,64]{0,1:T(8,128)} async-done(((f32[1024,64]{0,1:T(8,128)}), f32[1024,64]{0,1:T(8,128)}) %all-reduce.10.cloned.1.call-update) | async-done | bytes 262160 | tf_op jit(solution)/shard_map/psum | solution.py:95
  270.3 33.7 %all-reduce.12.cloned.1.call-done = f32[1024,64]{0,1:T(8,128)} async-done(((f32[1024,64]{0,1:T(8,128)}), f32[1024,64]{0,1:T(8,128)}) %all-reduce.12.cloned.1.call-update) | async-done | bytes 262160 | tf_op jit(solution)/shard_map/psum | solution.py:95
  303.9 1.6 convolution_bitcast_fusion.1
  305.7 6.9 %scatter_fusion.1 = f32[8,32,64]{2,1,0:T(8,128)S(1)} fusion(f32[8,32,64]{2,1,0:T(8,128)S(1)} %broadcast_in_dim.8, s32[128]{0:T(128)S(1)} %get-tuple-element.8, f32[128,64]{1,0:T(8,128)S(1)} %copy.27), kind=kCustom, calls=%fused_computation.5 | custom fusion | bytes 99328 | tf_op jit(solution)/shard_map/scatter | solution.py:103
  313.3 5.5 %all-to-all-start.2 = ((f32[8,1,2048]{2,1,0:T(1,128)}), f32[8,1,2048]{2,1,0:T(1,128)S(1)}, u32[]{:S(2)}, u32[]{:S(2)}) async-start(f32[8,1,2048]{2,1,0:T(1,128)} %reshape.116), calls=%async_computation.2 | async-start | bytes 131072 | tf_op jit(solution)/shard_map/all_to_all | solution.py:105
  318.9 6.9 %all-to-all-done.2 = f32[8,1,2048]{2,1,0:T(1,128)S(1)} async-done(((f32[8,1,2048]{2,1,0:T(1,128)}), f32[8,1,2048]{2,1,0:T(1,128)S(1)}, u32[]{:S(2)}, u32[]{:S(2)}) %all-to-all-start.2) | async-done | bytes 65568 | tf_op jit(solution)/shard_map/all_to_all | solution.py:105
  326.6 1.7 scatter_custom_fusion.2
  330.0 27.9 %all-reduce.14.cloned.1.call-done = f32[512,64]{0,1:T(8,128)} async-done(((f32[512,64]{0,1:T(8,128)}), f32[512,64]{0,1:T(8,128)}) %all-reduce.14.cloned.1.call-update) | async-done | bytes 131088 | tf_op jit(solution)/shard_map/psum | solution.py:107
  357.9 1.6 sub.38
  (61 shorter events, 8.8 us)
Async XLA Ops:
  7.2 194.2 %copy-start = (f32[128,1024]{1,0:T(8,128)S(1)}, f32[128,1024]{1,0:T(8,128)}, u32[]{:S(2)}) copy-start(f32[128,1024]{1,0:T(8,128)} %param.14) | copy-start | bytes 1572868
  7.2 0.7 copy-start.6
  8.3 0.7 copy-start.8
  9.0 27.4 %copy-start.3 = (f32[512,128]{1,0:T(8,128)S(1)}, f32[512,128]{1,0:T(8,128)}, u32[]{:S(2)}) copy-start(f32[512,128]{1,0:T(8,128)} %param.12) | copy-start | bytes 786436
  9.0 27.6 %copy-start.5 = (f32[1024,128]{1,0:T(8,128)S(1)}, f32[1024,128]{1,0:T(8,128)}, u32[]{:S(2)}) copy-start(f32[1024,128]{1,0:T(8,128)} %param.9) | copy-start | bytes 1572868
  28.9 7.5 %copy-start.9 = (s32[64]{0:T(128)S(1)}, s32[64]{0:T(128)}, u32[]{:S(2)}) copy-start(s32[64]{0:T(128)} %param.11) | copy-start | bytes 772
  28.9 82.3 %all-to-all-start = ((s32[8,1,32]{2,1,0:T(1,128)}), s32[8,1,32]{2,1,0:T(1,128)S(1)}, u32[]{:S(2)}, u32[]{:S(2)}) async-start(s32[8,1,32]{2,1,0:T(1,128)} %bitcast.4), calls=%async_computation | async-start | bytes 8192 | tf_op jit(solution)/shard_map/all_to_all | solution.py:84
  36.3 114.5 %all-reduce.6.cloned.1.call-start = ((), (), s32[]{:S(2)}) async-start(), calls=%async_computation.3 | async-start | bytes 262144 | tf_op jit(solution)/shard_map/psum | solution.py:64
  68.6 8.9 %copy-start.4 = (f32[512,64]{0,1:T(8,128)S(1)}, f32[512,64]{0,1:T(8,128)}, u32[]{:S(2)}) copy-start(f32[512,64]{0,1:T(8,128)} %param.13) | copy-start | bytes 393220
  77.5 1.9 copy-start.2
  79.4 105.2 %all-reduce.8.cloned.1.call-start = ((), (), s32[]{:S(2)}) async-start(), calls=%async_computation.4 | async-start | bytes 262144 | tf_op jit(solution)/shard_map/psum | solution.py:76
  153.2 117.0 %all-reduce.10.cloned.1.call-start = ((), (), s32[]{:S(2)}) async-start(), calls=%async_computation.5 | async-start | bytes 524288 | tf_op jit(solution)/shard_map/psum | solution.py:95
  202.5 101.4 %all-reduce.12.cloned.1.call-start = ((), (), s32[]{:S(2)}) async-start(), calls=%async_computation.6 | async-start | bytes 524288 | tf_op jit(solution)/shard_map/psum | solution.py:95
  270.2 33.7 %copy-start.7 = (f32[1024]{0:T(1024)S(1)}, f32[1024]{0:T(1024)}, u32[]{:S(2)}) copy-start(f32[1024]{0:T(1024)} %param.15) | copy-start | bytes 12292
  313.3 12.4 %all-to-all-start.2 = ((f32[8,1,2048]{2,1,0:T(1,128)}), f32[8,1,2048]{2,1,0:T(1,128)S(1)}, u32[]{:S(2)}, u32[]{:S(2)}) async-start(f32[8,1,2048]{2,1,0:T(1,128)} %reshape.116), calls=%async_computation.2 | async-start | bytes 131072 | tf_op jit(solution)/shard_map/all_to_all | solution.py:105
  318.8 39.0 %all-reduce.14.cloned.1.call-start = ((), (), s32[]{:S(2)}) async-start(), calls=%async_computation.7 | async-start | bytes 262144 | tf_op jit(solution)/shard_map/psum | solution.py:107
  329.1 28.7 %copy-start.1 = (f32[512,64]{0,1:T(8,128)S(1)}, f32[512,64]{0,1:T(8,128)}, u32[]{:S(2)}) copy-start(f32[512,64]{0,1:T(8,128)} %all-reduce.8.cloned.1.call-done) | copy-start | bytes 393220
Sparse Core Ops, SparseCore 0:
  79.5 71.2 all-reduce.5
  153.7 30.8 all-reduce.7
  202.6 67.5 all-reduce.9
  272.4 31.4 all-reduce.11
  329.3 28.5 all-reduce.13
